TPU v7x, 32 devices: a whole 2x2x4 slice. The times are simulated.
32 devices in a mesh: dp: 4 (over y, core), head: 8 (over z, x).
Axes of the slice: x: 2, y: 2, z: 4, core: 2. Of those that a mesh axis runs over, the one named last changes fastest.
Arguments:
- hidden: bfloat16 [12288, 4096], P('dp'), may hold values from -6 to 6
- weight: bfloat16 [2048, 4096], P('head'), may hold values from -0.09375 to 0.09375
- block_ids: int32 [48, 8], P('dp'), may hold values from 0 to 15, all different within a row
- targets: int32 [12288, 8], P('dp'), may hold values from 0 to 2047
Outputs:
- grad_hidden: bfloat16 [12288, 4096], P('dp', 'head')
- grad_weight: bfloat16 [2048, 4096], P('head', 'dp')
Inputs may be any that keep to these rules, and one draw needn't show every extreme that they name: `block_ids`: each row block lists 8 different label blocks; every label block is listed by some row block. `targets`: a row may repeat a label id.
All inputs are finite; a program needn't handle non-finite values.
Results may differ from a plain program's by a relative error of at most 0.014.
Values may be sent and summed in bfloat16 or wider, within the bound.
No kernel may reach another device: no remote copies, remote signals or barrier semaphores. Data moves between devices by JAX's collectives and lax.ppermute only.
A program may use at most 192 MiB of HBM per device.

v0:
```python
import jax
import jax.numpy as jnp
from jax import lax
from jax.sharding import PartitionSpec as P

BLOCK = 128


def local(hidden, weight, block_ids, targets):
    head_count = lax.axis_size("head")
    device = lax.axis_index("head")
    owned = weight.shape[0]
    per_device = owned // BLOCK
    row_blocks = block_ids.shape[0]
    block_rows = hidden.shape[0] // row_blocks
    first = device * per_device
    owned_ids = first + jnp.arange(per_device, dtype=jnp.int32)
    logits = jnp.einsum("rd,ld->rl", hidden, weight, preferred_element_type=jnp.float32)
    slot_match = block_ids[:, :, None] == owned_ids[None, None, :]
    listed = jnp.any(slot_match, axis=1)
    row_mask = jnp.broadcast_to(
        listed[:, None, :, None], (row_blocks, block_rows, per_device, BLOCK)
    )
    row_mask = row_mask.reshape(row_blocks * block_rows, owned)
    labels = first * BLOCK + jnp.arange(owned, dtype=jnp.int32)
    hits = jnp.any(targets[:, :, None] == labels[None, None, :], axis=1)
    signal = jax.nn.sigmoid(logits) - hits.astype(jnp.float32)
    grads = jnp.where(row_mask, signal, 0.0).astype(jnp.bfloat16)
    weight_part = jnp.einsum("rl,rd->ld", grads, hidden, preferred_element_type=jnp.float32)
    grad_weight = lax.psum_scatter(
        weight_part.astype(jnp.bfloat16), "dp", scatter_dimension=1, tiled=True
    )
    grads4 = grads.reshape(row_blocks, block_rows, per_device, BLOCK)
    picker = slot_match.astype(jnp.bfloat16)
    slot_local = jnp.einsum(
        "ikb,irbj->ikrj", picker, grads4, preferred_element_type=jnp.float32
    ).astype(jnp.bfloat16)
    slot_total = lax.psum(slot_local, "head").astype(jnp.float32).astype(jnp.bfloat16)
    columns = lax.all_to_all(weight, "head", split_axis=1, concat_axis=0, tiled=True)
    narrow = columns.shape[1]
    blocks3 = columns.reshape(per_device * head_count, BLOCK, narrow)
    chosen = blocks3[block_ids]
    terms = jnp.einsum("ikrj,ikjd->ikrd", slot_total, chosen, preferred_element_type=jnp.float32)
    groups = jnp.arange(head_count, dtype=jnp.int32)
    owner = ((block_ids // per_device)[:, :, None] == groups[None, None, :]).astype(jnp.float32)
    parts = jnp.einsum("iko,ikrd->iord", owner, terms, precision=lax.Precision.HIGHEST)
    rounded = lax.optimization_barrier(parts.astype(jnp.bfloat16))
    summed = jnp.sum(rounded.astype(jnp.float32), axis=1)
    grad_hidden = summed.reshape(row_blocks * block_rows, narrow).astype(jnp.bfloat16)
    return (grad_hidden, grad_weight)


def solution(mesh):
    return jax.shard_map(
        local,
        mesh=mesh,
        in_specs=(P("dp", None), P("head", None), P("dp", None), P("dp", None)),
        out_specs=(P("dp", "head"), P("head", "dp")),
        check_vma=False,
    )
```

profile of v0, /device:TPU:0, one launch (start us, length us, event | category | flops | bytes accessed | tf_op | source)
XLA Modules:
  0.0 421.9 jit_solution(15903401731539270005)
XLA Ops:
  8.0 0.0 all-reduce.2.cloned.1.call-start
  8.1 0.8 copy.35
  8.8 0.4 compare_reduce_fusion.1
  9.2 0.1 copy.36
  9.3 0.3 broadcast_in_dim.7
  9.7 0.5 copy.46
  10.2 1.8 copy.38
  12.0 1.4 copy.37
  13.3 17.2 %compare_reduce_fusion = pred[3072,256]{1,0:T(8,128)(4,1)S(1)} fusion(s32[256]{0:T(256)S(1)} %iota_add_fusion, s32[3072,8]{1,0:T(8,128)S(1)} %copy.37), kind=kLoop, calls=%fused_computation.3 | loop fusion | flops 11796480 | bytes 885760 | tf_op jit(solution)/shard_map/reduce_or | solution.py:26
  30.5 13.2 %fusion.12 = bf16[3072,256]{1,0:T(8,128)(2,1)S(1)} fusion(pred[3072,256]{1,0:T(32,128)(4,1)} %copy.38, bf16[3072,4096]{1,0:T(8,128)(2,1)} %param.4, bf16[256,4096]{1,0:T(8,128)(2,1)} %param.5, pred[3072,256]{1,0:T(8,128)(4,1)S(1)} %compare_reduce_fusion), kind=kOutput, calls=%fused_computation.14 | convolution fusion | flops 6447955968 | bytes 30408704 | tf_op jit(solution)/shard_map/rd,ld->rl/dot_general | solution.py:18
  43.7 0.0 copy-start.1
  43.7 0.4 reshape.32
  44.2 4.5 %convolution_convert_fusion.1 = bf16[12,8,256,128]{3,1,2,0:T(8,128)(2,1)} fusion(bf16[12,256,2,128]{3,2,1,0:T(2,128)(2,1)S(1)} %reshape.32, s32[12,8]{1,0:T(8,128)S(1)} %copy.35, s32[2]{0:T(128)S(1)} %iota_add_fusion.1), kind=kOutput, calls=%fused_computation.15 | convolution fusion | flops 15728832 | bytes 7864712 | tf_op jit(solution)/shard_map/ikb,irbj->ikrj/dot_general | solution.py:35
  48.7 0.0 all-reduce.2.cloned.1.call-update
  48.7 0.0 copy-done.1
  48.7 4.1 copy.39
  52.8 7.3 %all-to-all-start = ((bf16[256,8,512]{0,2,1:T(8,128)(2,1)}), bf16[256,8,512]{0,2,1:T(8,128)(2,1)S(1)}, u32[]{:S(2)}, u32[]{:S(2)}) async-start(bf16[256,8,512]{0,2,1:T(8,128)(2,1)} %bitcast.29), calls=%async_computation | async-start | bytes 4194304 | tf_op jit(solution)/shard_map/all_to_all | solution.py:39
  60.1 0.0 copy-start.2
  60.1 0.2 reduce-scatter.2.cloned.1.call-start
  60.3 13.1 %convolution_convert_fusion = bf16[256,4096]{1,0:T(8,128)(2,1)} fusion(bf16[3072,256]{1,0:T(8,128)(2,1)} %copy-done.1, bf16[3072,4096]{1,0:T(8,128)(2,1)} %param.4), kind=kOutput, calls=%fused_computation.7 | convolution fusion | flops 6443499520 | bytes 28835840 | tf_op jit(solution)/shard_map/rl,rd->ld/dot_general | solution.py:29
  73.5 0.0 reduce-scatter.2.cloned.1.call-update
  73.5 0.0 copy-done.2
  73.5 0.1 copy.34
  73.6 0.1 copy.41
  73.7 0.1 reshape.36
  73.8 84.4 %all-to-all-done = bf16[256,8,512]{0,2,1:T(8,128)(2,1)S(1)} async-done(((bf16[256,8,512]{0,2,1:T(8,128)(2,1)}), bf16[256,8,512]{0,2,1:T(8,128)(2,1)S(1)}, u32[]{:S(2)}, u32[]{:S(2)}) %all-to-all-start) | async-done | bytes 2097184 | tf_op jit(solution)/shard_map/all_to_all | solution.py:39
  158.1 0.0 copy-start
  158.1 1.3 copy-done
  159.5 2.9 copy.40
  162.3 6.7 %gather_fusion = bf16[96,128,512]{2,1,0:T(8,128)(2,1)} fusion(bf16[16,128,512]{2,1,0:T(8,128)(2,1)S(1)} %bitcast.26, s32[1024]{0:T(1024)S(1)} %pad_clamp_fusion), kind=kCustom, calls=%fused_computation | custom fusion | bytes 25166208 | tf_op jit(solution)/shard_map/gather | solution.py:42
  169.1 137.8 %all-reduce.2.cloned.1.call-done = bf16[12,8,256,128]{3,1,2,0:T(8,128)(2,1)} async-done(((bf16[12,8,256,128]{3,1,2,0:T(8,128)(2,1)}), bf16[12,8,256,128]{3,1,2,0:T(8,128)(2,1)}) %all-reduce.2.cloned.1.call-update) | async-done | bytes 6291472 | tf_op jit(solution)/shard_map/psum | solution.py:38
  306.9 24.0 %fusion.5 = f32[12,8,256,512]{3,2,1,0:T(8,128)} fusion(bf16[12,8,128,512]{3,2,1,0:T(8,128)(2,1)} %bitcast.27, bf16[12,8,256,128]{3,1,2,0:T(8,128)(2,1)} %all-reduce.2.cloned.1.call-done), kind=kOutput, calls=%fused_computation.5 | convolution fusion | flops 3221225472 | bytes 69206016 | tf_op jit(solution)/shard_map/ikrj,ikjd->ikrd/dot_general | solution.py:43
  330.9 61.9 %fusion.2 = bf16[12,8,256,512]{3,1,2,0:T(8,128)(2,1)} fusion(f32[12,8,256,512]{3,2,1,0:T(8,128)} %fusion.5, s32[12,8]{1,0:T(8,128)S(1)} %copy.34), kind=kOutput, calls=%fused_computation.4 | convolution fusion | flops 1220543232 | bytes 75497856 | tf_op jit(solution)/shard_map/iko,ikrd->iord/dot_general | solution.py:46
  392.8 21.7 %reduce_sum.12 = bf16[12,256,512]{2,1,0:T(8,128)(2,1)} reduce(bf16[12,8,256,512]{3,1,2,0:T(8,128)(2,1)} %fusion.2, bf16[]{:T(256)} %constant.32.clone.1), dimensions={1}, to_apply=%region_3.4 | reduce | flops 11010048 | bytes 28311554 | tf_op jit(solution)/shard_map/reduce_sum | solution.py:48
  414.5 0.0 reduce-scatter.2.cloned.1.call-done
  (4 shorter events, 0.0 us)
Async XLA Ops:
  8.0 298.9 %all-reduce.2.cloned.1.call-start = ((), (), s32[]{:S(2)}) async-start(), calls=%async_computation.2 | async-start | bytes 12582912 | tf_op jit(solution)/shard_map/psum | solution.py:38
  43.7 5.0 %copy-start.1 = (bf16[3072,256]{1,0:T(8,128)(2,1)}, bf16[3072,256]{1,0:T(8,128)(2,1)S(1)}, u32[]{:S(2)}) copy-start(bf16[3072,256]{1,0:T(8,128)(2,1)S(1)} %fusion.12) | copy-start | bytes 4718596
  52.8 105.3 %all-to-all-start = ((bf16[256,8,512]{0,2,1:T(8,128)(2,1)}), bf16[256,8,512]{0,2,1:T(8,128)(2,1)S(1)}, u32[]{:S(2)}, u32[]{:S(2)}) async-start(bf16[256,8,512]{0,2,1:T(8,128)(2,1)} %bitcast.29), calls=%async_computation | async-start | bytes 4194304 | tf_op jit(solution)/shard_map/all_to_all | solution.py:39
  60.1 13.4 %copy-start.2 = (s32[12,8]{0,1:T(8,128)S(1)}, s32[12,8]{0,1:T(8,128)}, u32[]{:S(2)}) copy-start(s32[12,8]{0,1:T(8,128)} %param.6) | copy-start | bytes 1156
  60.1 354.4 %reduce-scatter.2.cloned.1.call-start = ((), (), s32[]{:S(2)}) async-start(), calls=%async_computation.3 | async-start | bytes 2621440 | tf_op jit(solution)/shard_map/reduce_scatter | solution.py:30
  158.1 1.3 copy-start
Sparse Core Ops, SparseCore 0:
  48.9 257.9 all-reduce.1
Sparse Core Ops, SparseCore 1:
  73.6 32.3 reduce-scatter.1
where the time goes:
time: 423 us; the launch traced here: 422 us
  waiting for transfers between devices  222 us (52%)
  matrix products  117 us (28%)
  other arithmetic  39.2 us (9%)
  local copies, waits for them, and re-layouts  20.6 us (5%)
  between operations  15.6 us (4%)
  starting transfers between devices  7.54 us (2%)
    psum x1, waiting for transfers between devices, local(): lax.psum(slot_local, 'head').astype(jnp.float32).astype(jnp.bfloat16)  138 us
    all_to_all x1, waiting for transfers between devices, local(): lax.all_to_all(weight, 'head', split_axis=1, concat_axis=0, tiled=True)  84.4 us
    dot_general x1, matrix products, local(): jnp.einsum('iko,ikrd->iord', owner, terms, precision=lax.Precision.HIGHEST)  61.9 us
    dot_general x1, matrix products, local(): jnp.einsum('ikrj,ikjd->ikrd', slot_total, chosen, preferred_element_type=...  24 us
    reduce_sum x1, other arithmetic, local(): summed = jnp.sum(rounded.astype(jnp.float32), axis=1)  21.7 us
    reduce_or x1, other arithmetic, local(): hits = jnp.any(targets[:, :, None] == labels[None, None, :], axis=1)  17.2 us
    dot_general x1, matrix products, local(): jnp.einsum('rd,ld->rl', hidden, weight, preferred_element_type=jnp.float32)  13.2 us
    dot_general x1, matrix products, local(): jnp.einsum('rl,rd->ld', grads, hidden, preferred_element_type=jnp.float32)  13.1 us
  transfers between devices with their start and end apart: 3, of which 2 were waited for; matrix products, arithmetic and copies ran while one was open for 32% of the time, Pallas kernels for 0%

commit v1 on v0

--- a/solution.py
+++ b/solution.py
@@ -35,7 +35,9 @@
     slot_local = jnp.einsum(
         "ikb,irbj->ikrj", picker, grads4, preferred_element_type=jnp.float32
     ).astype(jnp.bfloat16)
-    slot_total = lax.psum(slot_local, "head").astype(jnp.float32).astype(jnp.bfloat16)
+    slot_total = (
+        jnp.sum(lax.all_gather(slot_local, "head"), axis=0).astype(jnp.float32).astype(jnp.bfloat16)
+    )
     columns = lax.all_to_all(weight, "head", split_axis=1, concat_axis=0, tiled=True)
     narrow = columns.shape[1]
     blocks3 = columns.reshape(per_device * head_count, BLOCK, narrow)

time: 423 us -> 1160 us (2.74)
  waiting for transfers between devices: 222 us -> 941 us
  other arithmetic: 39.2 us -> 59.2 us
    all_gather x0 -> x1, waiting for transfers between devices: none -> 884 us  [local(): lax.all_gather(slot_local, 'head')]
    psum x1 -> x0, waiting for transfers between devices: 138 us -> none  [local(): lax.psum(slot_local, 'head').astype(jnp.float32).astype(jnp.bfloat16)]
    all_to_all x1, waiting for transfers between devices: 84.4 us -> 56.3 us  [local(): lax.all_to_all(weight, 'head', split_axis=1, concat_axis=0, tiled=True)]
    reduce_sum x0 -> x1, other arithmetic: none -> 20 us  [local(): jnp.sum(lax.all_gather(slot_local, 'head'), axis=0).astype(jnp.float32)]
  transfers between devices with their start and end apart: 3 -> 3, of which waited for: 2 -> 2; matrix products, arithmetic and copies ran while one was open for 32% -> 13% of each run, Pallas kernels for 0% -> 0%
where the time goes in v1:
time: 1160 us
  waiting for transfers between devices  941 us (81%)
  matrix products  116 us (10%)
  other arithmetic  59.2 us (5%)
  local copies, waits for them, and re-layouts  24.9 us (2%)
  between operations  15.6 us (1%)
    all_gather x1, waiting for transfers between devices, local(): lax.all_gather(slot_local, 'head')  884 us
    dot_general x1, matrix products, local(): jnp.einsum('iko,ikrd->iord', owner, terms, precision=lax.Precision.HIGHEST)  61.9 us
    all_to_all x1, waiting for transfers between devices, local(): lax.all_to_all(weight, 'head', split_axis=1, concat_axis=0, tiled=True)  56.3 us
    dot_general x1, matrix products, local(): jnp.einsum('ikrj,ikjd->ikrd', slot_total, chosen, preferred_element_type=...  24 us
  transfers between devices with their start and end apart: 3, of which 2 were waited for; matrix products, arithmetic and copies ran while one was open for 13% of the time, Pallas kernels for 0%

profile of v1, /device:TPU:0, one launch (start us, length us, event | category | flops | bytes accessed | tf_op | source)
XLA Modules:
  0.0 1164.0 jit_solution(8509796233300316719)
XLA Ops:
  8.0 0.0 all-gather.3.cloned.1.call-start
  8.1 0.8 copy.36
  8.8 0.4 compare_reduce_fusion.1
  9.2 0.1 copy.37
  9.3 0.3 broadcast_in_dim.7
  9.7 0.5 copy.50
  10.2 1.8 copy.39
  12.0 1.4 copy.38
  13.3 17.2 %compare_reduce_fusion = pred[3072,256]{1,0:T(8,128)(4,1)S(1)} fusion(s32[256]{0:T(256)S(1)} %iota_add_fusion, s32[3072,8]{1,0:T(8,128)S(1)} %copy.38), kind=kLoop, calls=%fused_computation.3 | loop fusion | flops 11796480 | bytes 885760 | tf_op jit(solution)/shard_map/reduce_or | solution.py:26
  30.5 13.2 %fusion.10 = bf16[3072,256]{1,0:T(8,128)(2,1)S(1)} fusion(pred[3072,256]{1,0:T(32,128)(4,1)} %copy.39, bf16[3072,4096]{1,0:T(8,128)(2,1)} %param.4, bf16[256,4096]{1,0:T(8,128)(2,1)} %param.5, pred[3072,256]{1,0:T(8,128)(4,1)S(1)} %compare_reduce_fusion), kind=kOutput, calls=%fused_computation.12 | convolution fusion | flops 6447955968 | bytes 30408704 | tf_op jit(solution)/shard_map/rd,ld->rl/dot_general | solution.py:18
  43.7 0.0 copy-start.1
  43.7 0.4 reshape.32
  44.2 2.8 convolution_convert_fusion.1
  47.0 4.4 copy.40
  51.4 0.0 copy-done.1
  51.4 0.0 copy-start.2
  51.4 0.0 all-gather.3.cloned.1.call-update
  51.4 1.6 copy-done.2
  53.0 2.4 copy.42
  55.4 7.3 all-to-all-start
  62.7 0.0 copy-start.3
  62.7 0.2 reduce-scatter.2.cloned.1.call-start
  62.9 14.3 %convolution_convert_fusion = bf16[256,4096]{1,0:T(8,128)(2,1)} fusion(bf16[3072,256]{1,0:T(8,128)(2,1)} %copy-done.1, bf16[3072,4096]{1,0:T(8,128)(2,1)} %param.4), kind=kOutput, calls=%fused_computation.5 | convolution fusion | flops 6443499520 | bytes 28835840 | tf_op jit(solution)/shard_map/rl,rd->ld/dot_general | solution.py:29
  77.2 0.0 reduce-scatter.2.cloned.1.call-update
  77.2 0.0 copy-done.3
  77.2 0.1 copy.35
  77.3 0.1 copy.44
  77.4 0.1 reshape.36
  77.5 56.3 %all-to-all-done = bf16[256,8,512]{0,2,1:T(8,128)(2,1)S(1)} async-done(((bf16[256,8,512]{0,2,1:T(8,128)(2,1)}), bf16[256,8,512]{0,2,1:T(8,128)(2,1)S(1)}, u32[]{:S(2)}, u32[]{:S(2)}) %all-to-all-start) | async-done | bytes 2097184 | tf_op jit(solution)/shard_map/all_to_all | solution.py:41
  133.8 0.0 copy-start
  133.8 1.3 copy-done
  135.1 2.9 copy.43
  138.0 6.7 gather_fusion
  144.7 884.3 %all-gather.3.cloned.1.call-done = bf16[96,8,256,128]{3,2,1,0:T(8,128)(2,1)} async-done(((bf16[12,8,256,128]{3,2,1,0:T(8,128)(2,1)}), bf16[96,8,256,128]{3,2,1,0:T(8,128)(2,1)}) %all-gather.3.cloned.1.call-update) | async-done | bytes 50331664 | tf_op jit(solution)/shard_map/all_gather | solution.py:39
  1029.0 20.0 %reduce_sum.24 = bf16[12,8,256,128]{3,2,1,0:T(8,128)(2,1)} reduce(bf16[8,12,8,256,128]{4,3,2,1,0:T(8,128)(2,1)} %bitcast.29, bf16[]{:T(256)} %constant.32.clone.1), dimensions={0}, to_apply=%region_2.3 | reduce | flops 22020096 | bytes 56623104 | tf_op jit(solution)/shard_map/reduce_sum | solution.py:39
  1049.0 24.0 %fusion.18 = f32[12,8,256,512]{3,2,1,0:T(8,128)} fusion(bf16[12,8,256,128]{3,2,1,0:T(8,128)(2,1)} %reduce_sum.24, bf16[12,8,128,512]{3,2,1,0:T(8,128)(2,1)} %bitcast.30), kind=kOutput, calls=%fused_computation.32 | convolution fusion | flops 3221225472 | bytes 69206016 | tf_op jit(solution)/shard_map/ikrj,ikjd->ikrd/dot_general | solution.py:45
  1073.0 61.9 %fusion.2 = bf16[12,8,256,512]{3,1,2,0:T(8,128)(2,1)} fusion(f32[12,8,256,512]{3,2,1,0:T(8,128)} %fusion.18, s32[12,8]{1,0:T(8,128)S(1)} %copy.35), kind=kOutput, calls=%fused_computation.4 | convolution fusion | flops 1220543232 | bytes 75497856 | tf_op jit(solution)/shard_map/iko,ikrd->iord/dot_general | solution.py:48
  1134.9 21.7 %reduce_sum.25 = bf16[12,256,512]{2,1,0:T(8,128)(2,1)} reduce(bf16[12,8,256,512]{3,1,2,0:T(8,128)(2,1)} %fusion.2, bf16[]{:T(256)} %constant.32.clone.1), dimensions={1}, to_apply=%region_3.4 | reduce | flops 11010048 | bytes 28311554 | tf_op jit(solution)/shard_map/reduce_sum | solution.py:50
  1156.6 0.0 reduce-scatter.2.cloned.1.call-done
  (4 shorter events, 0.0 us)
Async XLA Ops:
  8.0 1021.0 %all-gather.3.cloned.1.call-start = ((), (), s32[]{:S(2)}) async-start(), calls=%async_computation.3 | async-start | bytes 56623104 | tf_op jit(solution)/shard_map/all_gather | solution.py:39
  43.7 7.6 copy-start.1
  51.4 1.6 copy-start.2
  55.4 78.4 %all-to-all-start = ((bf16[256,8,512]{0,2,1:T(8,128)(2,1)}), bf16[256,8,512]{0,2,1:T(8,128)(2,1)S(1)}, u32[]{:S(2)}, u32[]{:S(2)}) async-start(bf16[256,8,512]{0,2,1:T(8,128)(2,1)} %bitcast.32), calls=%async_computation | async-start | bytes 4194304 | tf_op jit(solution)/shard_map/all_to_all | solution.py:41
  62.7 14.5 %copy-start.3 = (s32[12,8]{0,1:T(8,128)S(1)}, s32[12,8]{0,1:T(8,128)}, u32[]{:S(2)}) copy-start(s32[12,8]{0,1:T(8,128)} %param.6) | copy-start | bytes 1156
  62.7 1093.9 %reduce-scatter.2.cloned.1.call-start = ((), (), s32[]{:S(2)}) async-start(), calls=%async_computation.2 | async-start | bytes 2621440 | tf_op jit(solution)/shard_map/reduce_scatter | solution.py:30
  133.8 1.3 copy-start
Sparse Core Ops, SparseCore 0:
  51.5 977.4 all-gather.2
Sparse Core Ops, SparseCore 1:
  77.3 32.4 reduce-scatter.1
